TPU v7x, 128 devices: a whole 4x4x4 slice. The times are simulated.
128 devices in a mesh: row: 16 (over x, z), col: 8 (over y, core).
Axes of the slice: x: 4, y: 4, z: 4, core: 2. Of those that a mesh axis runs over, the one named last changes fastest.
Arguments:
- hole_panel: bfloat16 [8192, 98304], P('row', 'col'), may hold values from -0.0546875 to 0.0546875
- amplitudes: bfloat16 [768, 98304], P(('row', 'col')), may hold values from -6 to 6
- row_sizes: int32 [8], replicated, may hold values from 1 to 2048, 8192 in all
- col_sizes: int32 [8], replicated, may hold values from 1 to 24576, 98304 in all
- pair_order: int32 [768], replicated, may hold values from 0 to 767, each once
Outputs:
- cycle_term: float32 [8192, 768], P('row', 'col')
Inputs may be any that keep to these rules, and one draw needn't show every extreme that they name: `row_sizes`: the rows of irrep g follow those of the irreps below g; the sizes sum to 8192, the largest is 2048. `col_sizes`: the indices of irrep g follow those of the irreps below g; the sizes sum to 98304, the largest is 24576. `pair_order`: each pair appears once.
All inputs are finite; a program needn't handle non-finite values.
Results may differ from a plain program's by a relative error of at most 0.0003.
Values may be sent and summed in bfloat16 or wider, within the bound.
No kernel may reach another device: no remote copies, remote signals or barrier semaphores. Data moves between devices by JAX's collectives and lax.ppermute only.
A program may use at most 192 MiB of HBM per device.

v0:
```python
import jax
import jax.numpy as jnp
from jax import lax
from jax.sharding import PartitionSpec as P


def irrep_labels(sizes, count, offset):
    position = offset + lax.iota(jnp.int32, count)
    bounds = jnp.cumsum(sizes)
    return jnp.sum((position[:, None] >= bounds[None, :]).astype(jnp.int32), axis=1)


def contract(masked, piece):
    numbers = (((1,), (1,)), ((), ()))
    return lax.dot_general(masked, piece, numbers, preferred_element_type=jnp.float32)


def on_device(hole_panel, amplitudes, row_sizes, col_sizes, pair_order):
    row_count, col_count = hole_panel.shape
    row_devices = lax.axis_size("row")
    col_devices = lax.axis_size("col")
    per_device = amplitudes.shape[0]
    pair_total = per_device * row_devices * col_devices
    row_irrep = irrep_labels(row_sizes, row_count, lax.axis_index("row") * row_count)
    col_irrep = irrep_labels(col_sizes, col_count, lax.axis_index("col") * col_count)
    masked = jnp.where(
        row_irrep[:, None] == col_irrep[None, :], hole_panel, jnp.zeros((), hole_panel.dtype)
    )
    split_rows = lax.all_to_all(amplitudes, "col", split_axis=1, concat_axis=0, tiled=True)
    stored = contract(masked, lax.all_gather(split_rows, "row", axis=0, tiled=True))
    logical = jnp.zeros((row_count, pair_total), jnp.float32).at[:, pair_order].set(stored)
    return lax.psum_scatter(logical, "col", scatter_dimension=1, tiled=True)


def solution(mesh):
    in_specs = (P("row", "col"), P(("row", "col"), None), P(), P(), P())
    out_specs = P("row", "col")
    return jax.shard_map(
        on_device, mesh=mesh, in_specs=in_specs, out_specs=out_specs, check_vma=False
    )
```

profile of v0, /device:TPU:0, one launch (start us, length us, event | category | flops | bytes accessed | tf_op | source)
XLA Modules:
  0.0 221.0 jit_solution(13136093127057807586)
XLA Ops:
  6.5 0.0 all-gather.2.cloned.1.call-start
  6.5 26.4 %all_to_all.19 = bf16[6,8,12288]{2,0,1:T(8,128)(2,1)S(1)} all-to-all(bf16[6,8,12288]{2,0,1:T(8,128)(2,1)} %bitcast.10), channel_id=1, replica_groups=mesh['row'=16,'col'=8] {'col'}, dimensions={1} | all-to-all | bytes 2359296 | tf_op jit(solution)/shard_map/all_to_all | solution.py:29
  32.9 0.0 copy-start.1
  32.9 0.0 copy-start.2
  32.9 0.0 copy-start
  32.9 1.3 all_to_all.17
  34.2 0.0 all-gather.2.cloned.1.call-update
  34.2 0.0 reduce-scatter.2.cloned.1.call-start
  34.3 0.0 copy-done.1
  34.3 0.2 reduce-window.17
  34.5 0.0 copy-done.2
  34.5 0.2 reduce-window.16
  34.7 0.1 convert_reduce_fusion.1
  34.8 0.2 convert_reduce_fusion
  34.9 0.0 copy-done
  35.0 121.9 %all-gather.2.cloned.1.call-done = bf16[768,12288]{1,0:T(8,128)(2,1)} async-done(((bf16[48,12288]{1,0:T(8,128)(2,1)}), bf16[768,12288]{1,0:T(8,128)(2,1)}) %all-gather.2.cloned.1.call-update) | async-done | bytes 18874384 | tf_op jit(solution)/shard_map/all_gather | solution.py:30
  156.9 17.6 %fusion.4 = f32[768,512]{0,1:T(8,128)S(1)} fusion(bf16[768,12288]{1,0:T(8,128)(2,1)} %all-gather.2.cloned.1.call-done, bf16[512,12288]{1,0:T(8,128)(2,1)} %param.5, s32[12288]{0:T(1024)S(1)} %convert_reduce_fusion, s32[512]{0:T(512)S(1)} %convert_reduce_fusion.1), kind=kOutput, calls=%fused_computation.6 | convolution fusion | flops 9676259328 | bytes 33081344 | tf_op jit(solution)/shard_map/dot_general | solution.py:15
  174.5 0.5 copy.10
  175.0 6.7 %scatter_custom_fusion = f32[512,768]{0,1:T(8,128)} fusion(s32[768]{0:T(1024)S(1)} %compare_select_fusion.4, f32[768,512]{1,0:T(8,128)S(1)} %copy.10, f32[]{:T(128)} %constant.9.clone.1), kind=kCustom, calls=%fused_computation.7 | custom fusion | bytes 1572868 | tf_op jit(solution)/shard_map/scatter | solution.py:31
  181.7 0.0 reduce-scatter.2.cloned.1.call-update
  181.7 32.5 %reduce-scatter.2.cloned.1.call-done = f32[512,96]{0,1:T(8,128)} async-done(((f32[512,768]{0,1:T(8,128)}), f32[512,96]{0,1:T(8,128)}) %reduce-scatter.2.cloned.1.call-update) | async-done | bytes 196624 | tf_op jit(solution)/shard_map/reduce_scatter | solution.py:32
  (3 shorter events, 0.0 us)
Async XLA Ops:
  6.5 150.3 %all-gather.2.cloned.1.call-start = ((), (), s32[]{:S(2)}) async-start(), calls=%async_computation.2 | async-start | bytes 20054016 | tf_op jit(solution)/shard_map/all_gather | solution.py:30
  32.9 1.4 copy-start.1
  32.9 1.6 copy-start.2
  32.9 2.1 copy-start
  34.2 180.0 %reduce-scatter.2.cloned.1.call-start = ((), (), s32[]{:S(2)}) async-start(), calls=%async_computation.3 | async-start | bytes 1769472 | tf_op jit(solution)/shard_map/reduce_scatter | solution.py:32
Sparse Core Ops, SparseCore 0:
  34.3 122.4 all-gather.1
  181.9 32.3 reduce-scatter.1
where the time goes:
time: 221 us
  waiting for transfers between devices  154 us (70%)
  blocking collectives  26.4 us (12%)
  matrix products  17.6 us (8%)
  between operations  13.5 us (6%)
  local copies, waits for them, and re-layouts  8.5 us (4%)
    all_gather x1, waiting for transfers between devices, on_device(): lax.all_gather(split_rows, 'row', axis=0, tiled=True)  122 us
    reduce_scatter x1, waiting for transfers between devices, on_device(): return lax.psum_scatter(logical, 'col', scatter_dimension=1, tiled=True)  32.5 us
    all_to_all x1, blocking collectives, on_device(): lax.all_to_all(amplitudes, 'col', split_axis=1, concat_axis=0, tiled=True)  26.4 us
    dot_general x1, matrix products, contract(): lax.dot_general(masked, piece, numbers, preferred_element_type=jnp.float32)  17.6 us
    scatter x1, local copies, waits for them, and re-layouts, on_device(): jnp.zeros((row_count, pair_total), jnp.float32).at[:, pair_order]  6.72 us
  transfers between devices with their start and end apart: 2, of which 2 were waited for; matrix products, arithmetic and copies ran while one was open for 0% of the time, Pallas kernels for 0%

commit v1 on v0

--- a/solution.py
+++ b/solution.py
@@ -2,6 +2,13 @@
 import jax.numpy as jnp
 from jax import lax
 from jax.sharding import PartitionSpec as P
+
+
+def all_by_exchange(value, mesh_axis, dim):
+    peers = lax.axis_size(mesh_axis)
+    blocks = jnp.stack([value for _ in range(peers)])
+    blocks = lax.all_to_all(blocks, mesh_axis, split_axis=0, concat_axis=0)
+    return jnp.concatenate(blocks, axis=dim)
 
 
 def irrep_labels(sizes, count, offset):
@@ -27,7 +34,7 @@
         row_irrep[:, None] == col_irrep[None, :], hole_panel, jnp.zeros((), hole_panel.dtype)
     )
     split_rows = lax.all_to_all(amplitudes, "col", split_axis=1, concat_axis=0, tiled=True)
-    stored = contract(masked, lax.all_gather(split_rows, "row", axis=0, tiled=True))
+    stored = contract(masked, all_by_exchange(split_rows, "row", 0))
     logical = jnp.zeros((row_count, pair_total), jnp.float32).at[:, pair_order].set(stored)
     return lax.psum_scatter(logical, "col", scatter_dimension=1, tiled=True)
 

time: 221 us -> 450 us (2.04)
  waiting for transfers between devices: 154 us -> 370 us
  starting transfers between devices: 0.04 us -> 8.1 us
  local copies, waits for them, and re-layouts: 8.5 us -> 14.4 us
    all_to_all x0 -> x1, waiting for transfers between devices: none -> 331 us  [all_by_exchange(): blocks = lax.all_to_all(blocks, mesh_axis, split_axis=0, concat_axis=0)]
    all_gather x1 -> x0, waiting for transfers between devices: 122 us -> none  [on_device(): lax.all_gather(split_rows, 'row', axis=0, tiled=True)]
    all_to_all x0 -> x1, starting transfers between devices: none -> 8.05 us  [all_by_exchange(): blocks = lax.all_to_all(blocks, mesh_axis, split_axis=0, concat_axis=0)]
    another operation x0 -> x2, local copies, waits for them, and re-layouts: none -> 7.22 us  [all_by_exchange(): blocks = jnp.stack([value for _ in range(peers)])]
    reduce_scatter x1, waiting for transfers between devices: 32.5 us -> 38.3 us  [on_device(): return lax.psum_scatter(logical, 'col', scatter_dimension=1, tiled=True)]
where the time goes in v1:
time: 450 us
  waiting for transfers between devices  370 us (82%)
  blocking collectives  26.4 us (6%)
  matrix products  17.6 us (4%)
  local copies, waits for them, and re-layouts  14.4 us (3%)
  between operations  13.5 us (3%)
  starting transfers between devices  8.1 us (2%)
    all_to_all x1, waiting for transfers between devices, all_by_exchange(): blocks = lax.all_to_all(blocks, mesh_axis, split_axis=0, concat_axis=0)  331 us
    reduce_scatter x1, waiting for transfers between devices, on_device(): return lax.psum_scatter(logical, 'col', scatter_dimension=1, tiled=True)  38.3 us
    all_to_all x1, blocking collectives, on_device(): lax.all_to_all(amplitudes, 'col', split_axis=1, concat_axis=0, tiled=True)  26.4 us
    dot_general x1, matrix products, contract(): lax.dot_general(masked, piece, numbers, preferred_element_type=jnp.float32)  17.6 us
  transfers between devices with their start and end apart: 2, of which 2 were waited for; matrix products, arithmetic and copies ran while one was open for 0% of the time, Pallas kernels for 0%

profile of v1, /device:TPU:0, one launch (start us, length us, event | category | flops | bytes accessed | tf_op | source)
XLA Modules:
  0.0 450.2 jit_solution(3165990990676124405)
XLA Ops:
  6.5 26.4 %all_to_all.21 = bf16[6,8,12288]{2,0,1:T(8,128)(2,1)S(1)} all-to-all(bf16[6,8,12288]{2,0,1:T(8,128)(2,1)} %bitcast.11), channel_id=1, replica_groups=mesh['row'=16,'col'=8] {'col'}, dimensions={1} | all-to-all | bytes 2359296 | tf_op jit(solution)/shard_map/all_to_all | solution.py:36
  32.9 0.5 stack.4
  33.4 6.8 %stack.5 = bf16[16,48,12288]{2,1,0:T(8,128)(2,1)} broadcast(bf16[48,12288]{1,0:T(8,128)(2,1)S(1)} %stack.4), dimensions={1,2} | broadcast | bytes 20054016 | tf_op jit(solution)/shard_map/stack | solution.py:9
  40.1 0.0 copy-start.1
  40.1 0.0 copy-start.2
  40.1 0.0 copy-start
  40.1 8.1 %all-to-all-start.1 = ((bf16[16,48,12288]{2,1,0:T(8,128)(2,1)}), bf16[16,48,12288]{2,1,0:T(8,128)(2,1)}, u32[]{:S(2)}, u32[]{:S(2)}) async-start(bf16[16,48,12288]{2,1,0:T(8,128)(2,1)} %stack.5), calls=%async_computation.1 | async-start | bytes 37748736 | tf_op jit(solution)/shard_map/all_to_all | solution.py:10
  48.2 0.0 reduce-scatter.2.cloned.1.call-start
  48.2 0.0 copy-done.1
  48.3 0.2 reduce-window.17
  48.4 0.0 copy-done.2
  48.4 0.2 reduce-window.16
  48.6 0.1 convert_reduce_fusion.1
  48.7 0.2 convert_reduce_fusion
  48.9 0.0 copy-done
  48.9 331.2 %all-to-all-done.1 = bf16[16,48,12288]{2,1,0:T(8,128)(2,1)} async-done(((bf16[16,48,12288]{2,1,0:T(8,128)(2,1)}), bf16[16,48,12288]{2,1,0:T(8,128)(2,1)}, u32[]{:S(2)}, u32[]{:S(2)}) %all-to-all-start.1) | async-done | bytes 18874400 | tf_op jit(solution)/shard_map/all_to_all | solution.py:10
  380.2 17.6 %fusion.4 = f32[768,512]{0,1:T(8,128)S(1)} fusion(bf16[768,12288]{1,0:T(8,128)(2,1)} %bitcast.6, bf16[512,12288]{1,0:T(8,128)(2,1)} %param.5, s32[12288]{0:T(1024)S(1)} %convert_reduce_fusion, s32[512]{0:T(512)S(1)} %convert_reduce_fusion.1), kind=kOutput, calls=%fused_computation.6 | convolution fusion | flops 9676259328 | bytes 33081344 | tf_op jit(solution)/shard_map/dot_general | solution.py:22
  397.8 0.5 copy.10
  398.3 6.7 %scatter_custom_fusion = f32[512,768]{0,1:T(8,128)} fusion(s32[768]{0:T(1024)S(1)} %compare_select_fusion.4, f32[768,512]{1,0:T(8,128)S(1)} %copy.10, f32[]{:T(128)} %constant.9.clone.1), kind=kCustom, calls=%fused_computation.7 | custom fusion | bytes 1572868 | tf_op jit(solution)/shard_map/scatter | solution.py:38
  405.0 0.0 reduce-scatter.2.cloned.1.call-update
  405.0 38.3 %reduce-scatter.2.cloned.1.call-done = f32[512,96]{0,1:T(8,128)} async-done(((f32[512,768]{0,1:T(8,128)}), f32[512,96]{0,1:T(8,128)}) %reduce-scatter.2.cloned.1.call-update) | async-done | bytes 196624 | tf_op jit(solution)/shard_map/reduce_scatter | solution.py:39
  (3 shorter events, 0.0 us)
Async XLA Ops:
  40.1 8.1 %copy-start.1 = (s32[8]{0:T(128)S(1)}, s32[8]{0:T(128)}, u32[]{:S(2)}) copy-start(s32[8]{0:T(128)} %param.8) | copy-start | bytes 100
  40.1 8.3 %copy-start.2 = (s32[8]{0:T(128)S(1)}, s32[8]{0:T(128)}, u32[]{:S(2)}) copy-start(s32[8]{0:T(128)} %param.7) | copy-start | bytes 100
  40.1 8.8 %copy-start = (s32[768]{0:T(1024)S(1)}, s32[768]{0:T(1024)}, u32[]{:S(2)}) copy-start(s32[768]{0:T(1024)} %param.9) | copy-start | bytes 9220
  40.1 340.1 %all-to-all-start.1 = ((bf16[16,48,12288]{2,1,0:T(8,128)(2,1)}), bf16[16,48,12288]{2,1,0:T(8,128)(2,1)}, u32[]{:S(2)}, u32[]{:S(2)}) async-start(bf16[16,48,12288]{2,1,0:T(8,128)(2,1)} %stack.5), calls=%async_computation.1 | async-start | bytes 37748736 | tf_op jit(solution)/shard_map/all_to_all | solution.py:10
  48.2 395.2 %reduce-scatter.2.cloned.1.call-start = ((), (), s32[]{:S(2)}) async-start(), calls=%async_computation.3 | async-start | bytes 1769472 | tf_op jit(solution)/shard_map/reduce_scatter | solution.py:39
Sparse Core Ops, SparseCore 0:
  405.2 38.1 reduce-scatter.1

commit v2 on v0

--- a/solution.py
+++ b/solution.py
@@ -2,6 +2,15 @@
 import jax.numpy as jnp
 from jax import lax
 from jax.sharding import PartitionSpec as P
+
+
+def handle_vectors(mine, peer_axis, dim_k, d_out):
+    piece_next = lax.axis_size(peer_axis)
+    kept_arr = jnp.split(mine, piece_next, axis=dim_k)
+    low = jnp.stack(kept_arr, axis=0)
+    work_now = lax.all_to_all(low, axis_name=peer_axis, split_axis=0, concat_axis=0)
+    value_now = jnp.concatenate(work_now, axis=d_out)
+    return value_now
 
 
 def irrep_labels(sizes, count, offset):
@@ -26,7 +35,7 @@
     masked = jnp.where(
         row_irrep[:, None] == col_irrep[None, :], hole_panel, jnp.zeros((), hole_panel.dtype)
     )
-    split_rows = lax.all_to_all(amplitudes, "col", split_axis=1, concat_axis=0, tiled=True)
+    split_rows = handle_vectors(amplitudes, "col", 1, 0)
     stored = contract(masked, lax.all_gather(split_rows, "row", axis=0, tiled=True))
     logical = jnp.zeros((row_count, pair_total), jnp.float32).at[:, pair_order].set(stored)
     return lax.psum_scatter(logical, "col", scatter_dimension=1, tiled=True)

time: 221 us -> 228 us (1.032)
  local copies, waits for them, and re-layouts: 8.5 us -> 15.6 us
    unnamed x6 -> x13, local copies, waits for them, and re-layouts: 0.01 us -> 6.61 us
where the time goes in v2:
time: 228 us
  waiting for transfers between devices  154 us (68%)
  blocking collectives  26.2 us (11%)
  matrix products  17.6 us (8%)
  local copies, waits for them, and re-layouts  15.6 us (7%)
  between operations  13.5 us (6%)
    all_gather x1, waiting for transfers between devices, on_device(): lax.all_gather(split_rows, 'row', axis=0, tiled=True)  122 us
    reduce_scatter x1, waiting for transfers between devices, on_device(): return lax.psum_scatter(logical, 'col', scatter_dimension=1, tiled=True)  32.5 us
    all_to_all x1, blocking collectives, handle_vectors(): lax.all_to_all(low, axis_name=peer_axis, split_axis=0, concat_axis=0)  26.2 us
    dot_general x1, matrix products, contract(): lax.dot_general(masked, piece, numbers, preferred_element_type=jnp.float32)  17.6 us
    scatter x1, local copies, waits for them, and re-layouts, on_device(): jnp.zeros((row_count, pair_total), jnp.float32).at[:, pair_order]  6.72 us
    unnamed x13, local copies, waits for them, and re-layouts  6.61 us
  transfers between devices with their start and end apart: 2, of which 2 were waited for; matrix products, arithmetic and copies ran while one was open for 0% of the time, Pallas kernels for 0%

profile of v2, /device:TPU:0, one launch (start us, length us, event | category | flops | bytes accessed | tf_op | source)
XLA Modules:
  0.0 228.0 jit_solution(15427910160815590159)
XLA Ops:
  6.5 0.0 all-gather.2.cloned.1.call-start
  6.5 0.9 bitcast_dynamic-update-slice_fusion.7
  7.5 0.9 bitcast_dynamic-update-slice_fusion.6
  8.4 0.9 bitcast_dynamic-update-slice_fusion.5
  9.4 0.9 bitcast_dynamic-update-slice_fusion.4
  10.3 0.9 bitcast_dynamic-update-slice_fusion.3
  11.3 0.9 bitcast_dynamic-update-slice_fusion.2
  12.2 0.9 bitcast_dynamic-update-slice_fusion.1
  13.2 0.9 bitcast_dynamic-update-slice_fusion
  14.1 26.2 %all_to_all.5 = bf16[8,6,12288]{2,1,0:T(8,128)(2,1)S(1)} all-to-all(bf16[8,6,12288]{2,1,0:T(8,128)(2,1)S(1)} %bitcast_dynamic-update-slice_fusion), channel_id=1, replica_groups=mesh['row'=16,'col'=8] {'col'}, dimensions={0} | all-to-all | bytes 2359296 | tf_op jit(solution)/shard_map/all_to_all | solution.py:11
  40.3 1.3 reshape.65
  41.6 0.0 all-gather.2.cloned.1.call-update
  41.6 0.0 reduce-scatter.2.cloned.1.call-start
  41.6 0.0 copy-done.1
  41.7 0.2 reduce-window.17
  41.8 0.0 copy-done.2
  41.8 0.2 reduce-window.16
  42.0 0.1 convert_reduce_fusion.1
  42.1 0.2 convert_reduce_fusion
  42.3 121.9 %all-gather.2.cloned.1.call-done = bf16[768,12288]{1,0:T(8,128)(2,1)} async-done(((bf16[48,12288]{1,0:T(8,128)(2,1)}), bf16[768,12288]{1,0:T(8,128)(2,1)}) %all-gather.2.cloned.1.call-update) | async-done | bytes 18874384 | tf_op jit(solution)/shard_map/all_gather | solution.py:39
  164.3 17.6 %fusion = f32[768,512]{1,0:T(8,128)S(1)} fusion(bf16[768,12288]{1,0:T(8,128)(2,1)} %all-gather.2.cloned.1.call-done, bf16[512,12288]{1,0:T(8,128)(2,1)} %param.5, s32[12288]{0:T(1024)S(1)} %convert_reduce_fusion, s32[512]{0:T(512)S(1)} %convert_reduce_fusion.1), kind=kOutput, calls=%fused_computation.2 | convolution fusion | flops 9676259328 | bytes 33081344 | tf_op jit(solution)/shard_map/dot_general | solution.py:24
  181.9 6.7 %scatter_custom_fusion = f32[512,768]{0,1:T(8,128)} fusion(s32[768]{0:T(1024)S(1)} %compare_select_fusion.2, f32[768,512]{1,0:T(8,128)S(1)} %fusion, f32[]{:T(128)} %constant.9.clone.1), kind=kCustom, calls=%fused_computation.6 | custom fusion | bytes 1572868 | tf_op jit(solution)/shard_map/scatter | solution.py:40
  188.6 0.0 reduce-scatter.2.cloned.1.call-update
  188.6 32.5 %reduce-scatter.2.cloned.1.call-done = f32[512,96]{0,1:T(8,128)} async-done(((f32[512,768]{0,1:T(8,128)}), f32[512,96]{0,1:T(8,128)}) %reduce-scatter.2.cloned.1.call-update) | async-done | bytes 196624 | tf_op jit(solution)/shard_map/reduce_scatter | solution.py:41
  (7 shorter events, 0.0 us)
Async XLA Ops:
  6.5 157.7 %all-gather.2.cloned.1.call-start = ((), (), s32[]{:S(2)}) async-start(), calls=%async_computation.2 | async-start | bytes 20054016 | tf_op jit(solution)/shard_map/all_gather | solution.py:39
  40.3 1.4 copy-start.1
  40.3 1.6 copy-start.2
  40.3 2.1 copy-start
  41.6 179.5 %reduce-scatter.2.cloned.1.call-start = ((), (), s32[]{:S(2)}) async-start(), calls=%async_computation.3 | async-start | bytes 1769472 | tf_op jit(solution)/shard_map/reduce_scatter | solution.py:41
Sparse Core Ops, SparseCore 0:
  41.7 122.4 all-gather.1
  188.7 32.3 reduce-scatter.1
